TPU v7x, 32 devices: a whole 2x2x4 slice. The times are simulated.
32 devices in a mesh: req: 4 (over z), head: 8 (over y, x, core).
Axes of the slice: x: 2, y: 2, z: 4, core: 2. Of those that a mesh axis runs over, the one named last changes fastest.
Arguments:
- hidden_in: bfloat16 [64, 1024], P(('req', 'head')), may hold values from -6 to 6
- lengths: int32 [64], P('req'), may hold values from 2 to 1024, as said below
- request_order: int32 [64], replicated, may hold values from 0 to 63, each once
- key_cache: bfloat16 [2, 64, 16, 64, 1024], P(None, 'req', 'head')
- value_cache: bfloat16 [2, 64, 16, 64, 1024], P(None, 'req', 'head'), may hold values from -6 to 6
- w_qkv: bfloat16 [2, 16, 1024, 192], P(None, 'head'), may hold values from -0.1875 to 0.1875
- w_out: bfloat16 [2, 16, 64, 1024], P(None, 'head'), may hold values from -0.1875 to 0.1875
- w_up: bfloat16 [2, 1024, 4096], P(None, None, ('req', 'head')), may hold values from -0.1875 to 0.1875
- bias_up: bfloat16 [2, 4096], P(None, ('req', 'head')), may hold values from -3 to 3
- w_down: bfloat16 [2, 1024, 4096], P(None, None, ('req', 'head')), may hold values from -0.09375 to 0.09375
- norm_gain: float32 [2, 2, 1024], replicated, may hold values from 0.1 to 1.9
- norm_bias: float32 [2, 2, 1024], replicated, may hold values from -3 to 3
- embedding: bfloat16 [49152, 1024], P(('req', 'head')), may hold values from -0.59765625 to 0.59765625
Outputs:
- logits: float32 [64, 49152], P(None, ('req', 'head'))
Inputs may be any that keep to these rules, and one draw needn't show every extreme that they name: `lengths`: the largest length is 1024. Slot s of the caches and of lengths belongs to request request_order[s]; each request once.
All inputs are finite; a program needn't handle non-finite values.
Results may differ from a plain program's by a relative error of at most 0.0095.
Values may be sent and summed in bfloat16 or wider, within the bound.
A program may use at most 64 MiB of HBM per device.

v0:
```python
import jax
import jax.numpy as jnp
from jax import lax
from jax.sharding import PartitionSpec as P

LAYERS = 2


def layer_norm(values, gain_vec, bias_vec):
    average = jnp.mean(values, axis=-1, keepdims=True)
    centred = values - average
    variance = jnp.mean(centred * centred, axis=-1, keepdims=True)
    return centred * lax.rsqrt(variance + 1e-05) * gain_vec + bias_vec


def body(
    hidden_in,
    lengths,
    request_order,
    key_cache,
    value_cache,
    w_qkv,
    w_out,
    w_up,
    bias_up,
    w_down,
    norm_gain,
    norm_bias,
    embedding,
):
    group_size = lengths.shape[0]
    row_share = hidden_in.shape[0]
    head_size = w_out.shape[2]
    score_scale = head_size ** (-0.5)
    positions = jnp.arange(key_cache.shape[-1], dtype=jnp.int32)
    valid = positions[None, None, :] < lengths[:, None, None]
    gathered = lax.all_gather(hidden_in, ("req", "head"), axis=0, tiled=True)
    slot_ids = lax.dynamic_slice_in_dim(
        request_order, lax.axis_index("req") * group_size, group_size, 0
    )
    group_rows = gathered[slot_ids]
    own_rows = lax.dynamic_slice_in_dim(
        group_rows, lax.axis_index("head") * row_share, row_share, 0
    )
    for layer_idx in range(LAYERS):
        if layer_idx > 0:
            group_rows = lax.all_gather(own_rows, "head", axis=0, tiled=True)
        projected = jnp.einsum(
            "rd,hde->rhe", group_rows, w_qkv[layer_idx], preferred_element_type=jnp.float32
        ).astype(jnp.bfloat16)
        query = projected[..., :head_size]
        own_key = projected[..., head_size : 2 * head_size]
        own_value = projected[..., 2 * head_size :]
        scores = (
            jnp.einsum(
                "rhd,rhdl->rhl", query, key_cache[layer_idx], preferred_element_type=jnp.float32
            )
            * score_scale
        )
        scores = jnp.where(valid, scores, -jnp.inf)
        own = (
            jnp.sum(query.astype(jnp.float32) * own_key.astype(jnp.float32), axis=-1) * score_scale
        )
        row_max = jnp.maximum(jnp.max(scores, axis=-1), own)
        expo = jnp.exp(scores - row_max[..., None])
        own_exp = jnp.exp(own - row_max)
        denom = jnp.sum(expo, axis=-1) + own_exp
        mixed = jnp.einsum(
            "rhl,rhdl->rhd",
            expo.astype(jnp.bfloat16),
            value_cache[layer_idx],
            preferred_element_type=jnp.float32,
        )
        mixed = mixed + own_exp.astype(jnp.bfloat16).astype(jnp.float32)[
            ..., None
        ] * own_value.astype(jnp.float32)
        head_out = (mixed / denom[..., None]).astype(jnp.bfloat16)
        out_weight = w_out[layer_idx]
        attn_out = lax.psum_scatter(
            jnp.einsum("rhd,hde->re", head_out, out_weight, preferred_element_type=jnp.float32),
            "head",
            scatter_dimension=0,
            tiled=True,
        )
        normed = layer_norm(
            own_rows.astype(jnp.float32) + attn_out,
            norm_gain[layer_idx, 0],
            norm_bias[layer_idx, 0],
        ).astype(jnp.bfloat16)
        up_local = w_up[layer_idx]
        bias_local = bias_up[layer_idx].astype(jnp.float32)
        down_local = w_down[layer_idx]
        pre_act = (
            jnp.dot(
                lax.all_gather(normed, ("req", "head"), axis=0, tiled=True),
                up_local,
                preferred_element_type=jnp.float32,
            )
            + bias_local
        )
        hidden = jax.nn.gelu(pre_act, approximate=False).astype(jnp.bfloat16)
        mlp_out = lax.psum_scatter(
            jnp.einsum("rf,df->rd", hidden, down_local, preferred_element_type=jnp.float32),
            ("req", "head"),
            scatter_dimension=0,
            tiled=True,
        )
        own_rows = layer_norm(
            normed.astype(jnp.float32) + mlp_out, norm_gain[layer_idx, 1], norm_bias[layer_idx, 1]
        ).astype(jnp.bfloat16)
    everything = lax.all_gather(own_rows, ("req", "head"), axis=0, tiled=True)
    inverse = (
        jnp.zeros_like(request_order)
        .at[request_order]
        .set(jnp.arange(request_order.shape[0], dtype=jnp.int32))
    )
    return jnp.dot(everything[inverse], embedding.T, preferred_element_type=jnp.float32)


def solution(mesh):
    placed = (
        P(("req", "head"), None),
        P("req"),
        P(),
        P(None, "req", "head", None, None),
        P(None, "req", "head", None, None),
        P(None, "head", None, None),
        P(None, "head", None, None),
        P(None, None, ("req", "head")),
        P(None, ("req", "head")),
        P(None, None, ("req", "head")),
        P(),
        P(),
        P(("req", "head"), None),
    )
    return jax.shard_map(
        body, mesh=mesh, in_specs=placed, out_specs=P(None, ("req", "head")), check_vma=False
    )
```

profile of v0, /device:TPU:0, one launch (start us, length us, event | category | flops | bytes accessed | tf_op | source)
XLA Modules:
  0.0 567.9 jit_solution(7226839117564876502)
XLA Ops:
  6.5 0.9 compare_select_fusion.2
  7.4 43.9 %all-gather = bf16[32,2,1024]{2,1,0:T(2,128)(2,1)S(1)} all-gather(bf16[1,2,1024]{2,1,0:T(2,128)(2,1)} %bitcast.134), channel_id=1, replica_groups=mesh['req'=4,'head'=8] {'req','head'}, dimensions={0}, use_global_device_ids=true | all-gather | bytes 135168 | tf_op jit(solution)/shard_map/all_gather | solution.py:37
  52.0 1.5 convolution_convert_fusion.1
  54.4 2.9 fusion.6
  57.7 3.4 fusion.4
  61.0 0.9 convolution_bitcast_fusion.1
  63.4 47.4 %all-reduce.9.cloned.1.call-done = f32[16,1024]{1,0:T(8,128)} async-done(((f32[16,1024]{1,0:T(8,128)}), f32[16,1024]{1,0:T(8,128)}) %all-reduce.9.cloned.1.call-update) | async-done | bytes 65552
  110.8 0.9 fusion.215
  111.7 1.0 multiply_reduce_fusion.5
  112.6 0.8 add_convert_fusion.3
  113.5 40.2 %all-gather.1 = bf16[32,2,1024]{2,1,0:T(2,128)(2,1)S(1)} all-gather(bf16[1,2,1024]{2,1,0:T(2,128)(2,1)S(1)} %bitcast.125), channel_id=1, replica_groups=mesh['req'=4,'head'=8] {'req','head'}, dimensions={0}, use_global_device_ids=true | all-gather | bytes 135168 | tf_op jit(solution)/shard_map/all_gather | solution.py:95
  153.8 2.1 fusion.20
  156.0 121.3 %all-reduce.11.cloned.1.call-done = f32[64,1024]{1,0:T(8,128)} async-done(((f32[64,1024]{1,0:T(8,128)}), f32[64,1024]{1,0:T(8,128)}) %all-reduce.11.cloned.1.call-update) | async-done | bytes 262160
  277.3 0.9 fusion.212
  278.2 0.9 multiply_reduce_fusion.4
  279.1 0.8 add_convert_fusion.2
  280.0 9.0 %all-gather.2 = bf16[8,2,1024]{2,1,0:T(2,128)(2,1)S(1)} all-gather(bf16[1,2,1024]{2,1,0:T(2,128)(2,1)S(1)} %bitcast.123), channel_id=1, replica_groups=mesh['req'=4,'head'=8] {'head'}, dimensions={0}, use_global_device_ids=true | all-gather | bytes 36864 | tf_op jit(solution)/shard_map/all_gather | solution.py:47
  289.0 1.4 convolution_convert_fusion
  290.6 2.9 fusion.2
  293.9 3.4 fusion
  297.2 0.9 convolution_bitcast_fusion
  299.1 50.7 %all-reduce.13.cloned.1.call-done = f32[16,1024]{1,0:T(8,128)} async-done(((f32[16,1024]{1,0:T(8,128)}), f32[16,1024]{1,0:T(8,128)}) %all-reduce.13.cloned.1.call-update) | async-done | bytes 65552
  349.8 0.9 fusion.213
  350.7 0.9 multiply_reduce_fusion.3
  351.6 0.8 add_convert_fusion.1
  352.5 40.2 %all-gather.3 = bf16[32,2,1024]{2,1,0:T(2,128)(2,1)S(1)} all-gather(bf16[1,2,1024]{2,1,0:T(2,128)(2,1)S(1)} %bitcast.124), channel_id=1, replica_groups=mesh['req'=4,'head'=8] {'req','head'}, dimensions={0}, use_global_device_ids=true | all-gather | bytes 135168 | tf_op jit(solution)/shard_map/all_gather | solution.py:95
  392.7 2.1 fusion.16
  394.9 121.3 %all-reduce.15.cloned.1.call-done = f32[64,1024]{1,0:T(8,128)} async-done(((f32[64,1024]{1,0:T(8,128)}), f32[64,1024]{1,0:T(8,128)}) %all-reduce.15.cloned.1.call-update) | async-done | bytes 262160
  516.2 0.9 fusion.214
  517.1 0.9 multiply_reduce_fusion.2
  518.9 39.9 %all-gather.4 = bf16[32,2,1024]{2,1,0:T(2,128)(2,1)S(1)} all-gather(bf16[1,2,1024]{2,1,0:T(2,128)(2,1)S(1)} %fusion.147), channel_id=1, replica_groups=mesh['req'=4,'head'=8] {'req','head'}, dimensions={0}, use_global_device_ids=true | all-gather | bytes 135168 | tf_op jit(solution)/shard_map/all_gather | solution.py:111
  559.5 1.8 fusion.218
  (63 shorter events, 5.8 us)
Async XLA Ops:
  6.5 553.0 %copy-start = (bf16[1536,1024]{1,0:T(8,128)(2,1)S(1)}, bf16[1536,1024]{1,0:T(8,128)(2,1)}, u32[]{:S(2)}) copy-start(bf16[1536,1024]{1,0:T(8,128)(2,1)} %param.25) | copy-start | bytes 9437188
  6.5 104.2 %all-reduce.9.cloned.1.call-start = ((), (), s32[]{:S(2)}) async-start(), calls=%async_computation | async-start | bytes 131072
  54.4 6.7 %copy-start.4 = (bf16[2,2,64,1024]{3,2,1,0:T(8,128)(2,1)S(1)}, bf16[2,2,64,1024]{3,2,1,0:T(8,128)(2,1)}, u32[]{:S(2)}) copy-start(bf16[2,2,64,1024]{3,2,1,0:T(8,128)(2,1)} %param.19) | copy-start | bytes 1572868
  54.4 7.7 %copy-start.1 = (f32[2,2,1024]{2,1,0:T(2,128)S(1)}, f32[2,2,1024]{2,1,0:T(2,128)}, u32[]{:S(2)}) copy-start(f32[2,2,1024]{2,1,0:T(2,128)} %param.23) | copy-start | bytes 49156
  54.4 7.7 %copy-start.2 = (f32[2,2,1024]{2,1,0:T(2,128)S(1)}, f32[2,2,1024]{2,1,0:T(2,128)}, u32[]{:S(2)}) copy-start(f32[2,2,1024]{2,1,0:T(2,128)} %param.24) | copy-start | bytes 49156
  54.4 7.7 %copy-start.3 = (bf16[2,128]{1,0:T(2,128)(2,1)S(1)}, bf16[2,128]{1,0:T(2,128)(2,1)}, u32[]{:S(2)}) copy-start(bf16[2,128]{1,0:T(2,128)(2,1)} %param.21) | copy-start | bytes 1540
  54.4 7.7 %copy-start.7 = (u32[32]{0:T(128)S(1)}, u32[32]{0:T(128)}, u32[]{:S(2)}) copy-start(u32[32]{0:T(128)} %constant.105) | copy-start | bytes 388
  62.0 215.3 %all-reduce.11.cloned.1.call-start = ((), (), s32[]{:S(2)}) async-start(), calls=%async_computation.1 | async-start | bytes 524288
  155.9 193.8 %all-reduce.13.cloned.1.call-start = ((), (), s32[]{:S(2)}) async-start(), calls=%async_computation.2 | async-start | bytes 131072
  290.6 6.6 %copy-start.5 = (bf16[2,2,64,1024]{3,2,1,0:T(8,128)(2,1)S(1)}, bf16[2,2,64,1024]{3,2,1,0:T(8,128)(2,1)}, u32[]{:S(2)}) copy-start(bf16[2,2,64,1024]{3,2,1,0:T(8,128)(2,1)} %param.19) | copy-start | bytes 1572868
  290.6 7.6 %copy-start.6 = (s32[64]{0:T(128)S(1)}, s32[64]{0:T(128)}, u32[]{:S(2)}) copy-start(s32[64]{0:T(128)} %param.15) | copy-start | bytes 772
  298.2 218.0 %all-reduce.15.cloned.1.call-start = ((), (), s32[]{:S(2)}) async-start(), calls=%async_computation.3 | async-start | bytes 524288
Sparse Core Ops, SparseCore 0:
  62.1 48.6 all-reduce.8
  156.0 121.1 all-reduce.10
  298.3 51.4 all-reduce.12
  395.0 121.1 all-reduce.14
where the time goes:
time: 569 us; the launch traced here: 568 us
  waiting for transfers between devices  341 us (60%)
  blocking collectives  173 us (30%)
  matrix products  23.4 us (4%)
  between operations  14 us (2%)
  other arithmetic  13.4 us (2%)
    unnamed x8, waiting for transfers between devices  341 us
    all_gather x2, blocking collectives, body(): lax.all_gather(normed, ('req', 'head'), axis=0, tiled=True)  80.5 us
    all_gather x1, blocking collectives, body(): gathered = lax.all_gather(hidden_in, ('req', 'head'), axis=0, tiled=True)  43.9 us
    all_gather x1, blocking collectives, body(): everything = lax.all_gather(own_rows, ('req', 'head'), axis=0, tiled=True)  39.9 us
  transfers between devices with their start and end apart: 4, of which 4 were waited for; matrix products, arithmetic and copies ran while one was open for 0% of the time, Pallas kernels for 0%

commit v1 on v0

v1 whole, which is shorter than its diff:
```python
import functools

import jax
import jax.numpy as jnp
from jax import lax
from jax.experimental import pallas as pl
from jax.experimental.pallas import tpu as pltpu
from jax.sharding import PartitionSpec as P

LAYERS = 2
MESH = pl.DeviceIdType.MESH
F32 = jnp.float32
BF16 = jnp.bfloat16
NT = (((1,), (1,)), ((), ()))


def layer_norm(values, gain_vec, bias_vec):
    average = jnp.mean(values, axis=-1, keepdims=True)
    centred = values - average
    variance = jnp.mean(centred * centred, axis=-1, keepdims=True)
    return centred * lax.rsqrt(variance + 1e-05) * gain_vec + bias_vec


def kernel(
    n_req,
    n_head,
    hidden_ref,
    lengths_ref,
    order_ref,
    key_hbm,
    value_hbm,
    qkv_hbm,
    out_w_hbm,
    up_hbm,
    bias_up_ref,
    down_hbm,
    gain_ref,
    bias_ref,
    emb_hbm,
    logits_ref,
    key_v,
    value_v,
    qkv_v,
    out_w_v,
    up_v,
    down_v,
    emb_v,
    load_sem,
    emb_sem,
    stage,
    column,
    plane,
    spread,
    column_send,
    column_recv,
    plane_send,
    plane_recv,
    spread_send,
    spread_recv,
):
    me_r = lax.axis_index("req")
    me_h = lax.axis_index("head")
    rows, width = hidden_ref.shape
    group, heads, head_size, cached = key_v.shape[1:]
    slots = n_req * group

    barrier = pltpu.get_barrier_semaphore()
    for step in range(1, n_head):
        peer = lax.rem(me_h + step, n_head)
        pl.semaphore_signal(barrier, inc=1, device_id=(me_r, peer), device_id_type=MESH)
    for step in range(1, n_req):
        peer = lax.rem(me_r + step, n_req)
        pl.semaphore_signal(barrier, inc=1, device_id=(peer, me_h), device_id_type=MESH)

    pairs = ((qkv_hbm, qkv_v), (key_hbm, key_v), (value_hbm, value_v), (out_w_hbm, out_w_v), (up_hbm, up_v), (down_hbm, down_v))

    def load(layer, which):
        source, target = pairs[which]
        return pltpu.make_async_copy(source.at[layer], target.at[layer], load_sem.at[layer, which])

    for layer in range(LAYERS):
        for which in range(len(pairs)):
            load(layer, which).start()
    emb_load = pltpu.make_async_copy(emb_hbm, emb_v, emb_sem)
    emb_load.start()

    def sum_column(turn, partial):
        stage[turn] = partial.astype(BF16).reshape(n_req, group, width)
        copies = []
        for step in range(1, n_req):
            peer = lax.rem(me_r + step, n_req)
            copies.append(
                pltpu.make_async_remote_copy(
                    src_ref=stage.at[turn, peer],
                    dst_ref=column.at[turn, step - 1],
                    send_sem=column_send.at[turn, step - 1],
                    recv_sem=column_recv.at[turn, step - 1],
                    device_id=(peer, me_h),
                    device_id_type=MESH,
                )
            )
        for copy in copies:
            copy.start()
        total = stage[turn, me_r].astype(F32)
        for step, copy in enumerate(copies):
            copy.wait()
            total += column[turn, step].astype(F32)
        return total

    def sum_plane(turn, partial):
        plane[turn, me_h] = partial.astype(BF16)
        copies = []
        for step in range(1, n_head):
            peer = lax.rem(me_h + step, n_head)
            copies.append(
                pltpu.make_async_remote_copy(
                    src_ref=plane.at[turn, me_h],
                    dst_ref=plane.at[turn, me_h],
                    send_sem=plane_send.at[turn, step - 1],
                    recv_sem=plane_recv.at[turn, step - 1],
                    device_id=(me_r, peer),
                    device_id_type=MESH,
                )
            )
        for copy in copies:
            copy.start()
        for copy in copies:
            copy.wait()
        total = plane[turn, 0].astype(F32)
        for peer in range(1, n_head):
            total += plane[turn, peer].astype(F32)
        return total

    def gather_column(turn, mine):
        spread[turn, me_r] = mine
        copies = []
        for step in range(1, n_req):
            peer = lax.rem(me_r + step, n_req)
            copies.append(
                pltpu.make_async_remote_copy(
                    src_ref=spread.at[turn, me_r],
                    dst_ref=spread.at[turn, me_r],
                    send_sem=spread_send.at[turn, step - 1],
                    recv_sem=spread_recv.at[turn, step - 1],
                    device_id=(peer, me_h),
                    device_id_type=MESH,
                )
            )
        for copy in copies:
            copy.start()
        for copy in copies:
            copy.wait()
        return spread[turn].reshape(slots, width)

    order_row = order_ref[...]
    eye = lax.broadcasted_iota(jnp.int32, (slots, slots), 0) == lax.broadcasted_iota(
        jnp.int32, (slots, slots), 1
    )
    order_col = jnp.sum(
        jnp.where(eye, jnp.broadcast_to(order_row, (slots, slots)).astype(F32), 0.0), axis=1, keepdims=True
    )
    first_row = (me_r * n_head + me_h) * rows
    hidden = hidden_ref[...].astype(F32)
    placed = jnp.zeros((slots, width), F32)
    for row in range(rows):
        placed = jnp.where(
            order_col == (first_row + row).astype(F32),
            jnp.broadcast_to(hidden[row : row + 1, :], (slots, width)),
            placed,
        )

    pl.semaphore_wait(barrier, n_head + n_req - 2)
    state = sum_plane(0, sum_column(0, placed)).astype(BF16)

    row_ids = lax.broadcasted_iota(jnp.int32, (group, cached), 0)
    limit = jnp.zeros((group, cached), jnp.int32)
    for row in range(group):
        limit = jnp.where(row_ids == row, lengths_ref[row], limit)
    valid = lax.broadcasted_iota(jnp.int32, (group, cached), 1) < limit
    flat = group * head_size
    diagonal = lax.broadcasted_iota(jnp.int32, (group, flat), 0) == (
        lax.broadcasted_iota(jnp.int32, (group, flat), 1) // head_size
    )
    score_scale = head_size ** (-0.5)

    def layer_step(layer, state):
        load(layer, 0).wait()
        attn = jnp.zeros((group, width), F32)
        parts = []
        for head in range(heads):
            projected = jnp.dot(state, qkv_v[layer, head], preferred_element_type=F32).astype(BF16).astype(F32)
            parts.append(
                (
                    projected[:, :head_size],
                    projected[:, head_size : 2 * head_size],
                    projected[:, 2 * head_size :],
                )
            )
        load(layer, 1).wait()
        expos = []
        for head in range(heads):
            query, own_key, own_value = parts[head]
            tiled = jnp.where(diagonal, jnp.concatenate([query] * group, axis=1), 0.0).astype(BF16)
            keys = key_v[layer, :, head].reshape(flat, cached)
            scores = jnp.dot(tiled, keys, preferred_element_type=F32) * score_scale
            scores = jnp.where(valid, scores, -jnp.inf)
            own = jnp.sum(query * own_key, axis=-1, keepdims=True) * score_scale
            row_max = jnp.maximum(jnp.max(scores, axis=-1, keepdims=True), own)
            expo = jnp.exp(scores - row_max)
            own_exp = jnp.exp(own - row_max)
            denom = jnp.sum(expo, axis=-1, keepdims=True) + own_exp
            expos.append((expo.astype(BF16), own_exp.astype(BF16).astype(F32), denom))
        load(layer, 2).wait()
        load(layer, 3).wait()
        for head in range(heads):
            expo, own_exp, denom = expos[head]
            values = value_v[layer, :, head].reshape(flat, cached)
            every = lax.dot_general(expo, values, NT, preferred_element_type=F32)
            every = jnp.where(diagonal, every, 0.0)
            mixed = every[:, :head_size]
            for part in range(1, group):
                mixed += every[:, part * head_size : (part + 1) * head_size]
            mixed += own_exp * parts[head][2]
            head_out = (mixed / denom).astype(BF16)
            attn += jnp.dot(head_out, out_w_v[layer, head], preferred_element_type=F32)
        attn = sum_plane(1 + 2 * layer, attn)
        gains, biases = gain_ref[layer], bias_ref[layer]
        normed = layer_norm(state.astype(F32) + attn, gains[0:1], biases[0:1]).astype(BF16)
        everyone = gather_column(layer, normed)
        load(layer, 4).wait()
        bias_up = bias_up_ref[...].astype(F32)
        bias_row = bias_up[0:1]
        for other in range(1, LAYERS):
            bias_row = jnp.where(layer == other, bias_up[other : other + 1], bias_row)
        pre_act = jnp.dot(everyone, up_v[layer], preferred_element_type=F32) + bias_row
        hidden = (0.5 * pre_act * (1.0 + lax.erf(pre_act * 0.7071067811865476))).astype(BF16)
        load(layer, 5).wait()
        mlp = lax.dot_general(hidden, down_v[layer], NT, preferred_element_type=F32)
        mlp = sum_plane(2 + 2 * layer, sum_column(1 + layer, mlp))
        return layer_norm(normed.astype(F32) + mlp, gains[1:2], biases[1:2]).astype(BF16)

    state = lax.fori_loop(0, LAYERS, layer_step, state)
    everyone = gather_column(LAYERS, state)
    pick = (lax.broadcasted_iota(jnp.int32, (slots, slots), 0) == jnp.broadcast_to(order_row, (slots, slots))).astype(
        F32
    ).astype(BF16)
    ordered = jnp.dot(pick, everyone, preferred_element_type=F32).astype(BF16)
    emb_load.wait()
    logits_ref[...] = lax.dot_general(ordered, emb_v[...], NT, preferred_element_type=F32)


def body(n_req, n_head, *args):
    (hidden_in, lengths, request_order, key_cache, value_cache, w_qkv, w_out, w_up, bias_up, w_down) = args[:10]
    norm_gain, norm_bias, embedding = args[10:]
    group = lengths.shape[0]
    width = hidden_in.shape[1]
    slots = request_order.shape[0]
    vmem = pl.BlockSpec(memory_space=pltpu.VMEM)
    smem = pl.BlockSpec(memory_space=pltpu.SMEM)
    hbm = pl.BlockSpec(memory_space=pl.ANY)
    dma = pltpu.SemaphoreType.DMA
    held = [key_cache, value_cache, w_qkv, w_out, w_up, w_down, embedding]
    return pl.pallas_call(
        functools.partial(kernel, n_req, n_head),
        out_shape=jax.ShapeDtypeStruct((slots, embedding.shape[0]), F32),
        in_specs=[vmem, smem, vmem, hbm, hbm, hbm, hbm, hbm, vmem, hbm, vmem, vmem, hbm],
        out_specs=vmem,
        scratch_shapes=[pltpu.VMEM(array.shape, array.dtype) for array in held]
        + [
            dma((LAYERS, 6)),
            dma,
            pltpu.VMEM((1 + LAYERS, n_req, group, width), BF16),
            pltpu.VMEM((1 + LAYERS, n_req - 1, group, width), BF16),
            pltpu.VMEM((1 + 2 * LAYERS, n_head, group, width), BF16),
            pltpu.VMEM((1 + LAYERS, n_req, group, width), BF16),
            dma((1 + LAYERS, n_req - 1)),
            dma((1 + LAYERS, n_req - 1)),
            dma((1 + 2 * LAYERS, n_head - 1)),
            dma((1 + 2 * LAYERS, n_head - 1)),
            dma((1 + LAYERS, n_req - 1)),
            dma((1 + LAYERS, n_req - 1)),
        ],
        compiler_params=pltpu.CompilerParams(
            collective_id=0, has_side_effects=True, vmem_limit_bytes=56 * 1024 * 1024
        ),
    )(
        hidden_in,
        lengths,
        request_order.reshape(1, slots),
        key_cache,
        value_cache,
        w_qkv,
        w_out,
        w_up,
        bias_up,
        w_down,
        norm_gain,
        norm_bias,
        embedding,
    )


def solution(mesh):
    placed = (
        P(("req", "head"), None),
        P("req"),
        P(),
        P(None, "req", "head", None, None),
        P(None, "req", "head", None, None),
        P(None, "head", None, None),
        P(None, "head", None, None),
        P(None, None, ("req", "head")),
        P(None, ("req", "head")),
        P(None, None, ("req", "head")),
        P(),
        P(),
        P(("req", "head"), None),
    )
    return jax.shard_map(
        functools.partial(body, mesh.shape["req"], mesh.shape["head"]),
        mesh=mesh,
        in_specs=placed,
        out_specs=P(None, ("req", "head")),
        check_vma=False,
    )
```

time: 569 us -> 69.6 us (0.12)
  waiting for transfers between devices: 341 us -> 0 us
  blocking collectives: 173 us -> 0 us
  Pallas kernels: 0 us -> 63.8 us
  matrix products: 23.4 us -> 0 us
  between operations: 14 us -> 0.01 us
  other arithmetic: 13.4 us -> 0 us
    unnamed x8 -> x0, waiting for transfers between devices: 341 us -> none
    all_gather x5 -> x0, blocking collectives: 173 us -> none  [the longest x2 80.5 us: body(): lax.all_gather(normed, ('req', 'head'), axis=0, tiled=True)]
    pallas_call x0 -> x1, Pallas kernels: none -> 63.8 us  [body(): pl.pallas_call(functools.partial(kernel, n_req, n_head), out_shape=jax.Sh...]
    dot_general x11 -> x0, matrix products: 23.4 us -> none  [the longest x2 6.76 us: body(): jnp.einsum('rhl,rhdl->rhd', expo.astype(jnp.bfloat16), value_cache[layer_...]
    reduce_sum x12 -> x0, other arithmetic: 8.05 us -> none  [the longest x4 3.8 us: layer_norm(): variance = jnp.mean(centred * centred, axis=-1, keepdims=True)]
  transfers between devices with their start and end apart: 4 -> 0, of which waited for: 4 -> 0; matrix products, arithmetic and copies ran while one was open for 0% -> 0% of each run, Pallas kernels for 0% -> 0%
where the time goes in v1:
time: 69.6 us; the launch traced here: 69.4 us
  Pallas kernels  63.8 us (92%)
  local copies, waits for them, and re-layouts  5.52 us (8%)
    pallas_call x1, Pallas kernels, body(): pl.pallas_call(functools.partial(kernel, n_req, n_head), out_shape=jax.Sh...  63.8 us
    unnamed x2, local copies, waits for them, and re-layouts  5.52 us

profile of v1, /device:TPU:0, one launch (start us, length us, event | category | flops | bytes accessed | tf_op | source)
XLA Modules:
  0.0 69.4 jit_solution(2632111741006353892)
XLA Ops:
  0.0 3.8 %copy.14.qkv_hbm = bf16[2,2,1024,192]{3,2,1,0:T(8,128)(2,1)} copy(bf16[2,2,1024,192]{2,3,1,0:T(8,128)(2,1)} %param.18) | data formatting | bytes 3145728 | tf_op args[5]
  3.8 63.8 %shard_map.127 = f32[64,1536]{1,0:T(8,128)} custom-call(bf16[2,1024]{1,0:T(2,128)(2,1)} %hidden_ref.1, s32[16]{0:T(128)} %lengths_ref.1, s32[1,64]{1,0:T(1,128)} %bitcast.1, bf16[2,16,2,64,1024]{4,3,2,1,0:T(8,128)(2,1)} %key_hbm.1, bf16[2,16,2,64,1024]{4,3,2,1,0:T(8,128)(2,1)} %value_hbm.1, bf16[2,2,1024,192]{3,2,1,0:T(8,128)(2,1)} %copy.14.qkv_hbm, ...), custom_call_target="tpu_custom_call" | custom-call | tf_op jit(solution)/shard_map/pallas_call | solution.py:263
  67.6 1.8 %copy.16 = f32[64,1536]{1,0:T(8,128)} copy(f32[64,1536]{1,0:T(8,128)} %shard_map.127) | data formatting | bytes 786432

commit v2 on v1

v2 whole, which is shorter than its diff:
```python
import functools

import jax
import jax.numpy as jnp
from jax import lax
from jax.experimental import pallas as pl
from jax.experimental.pallas import tpu as pltpu
from jax.sharding import PartitionSpec as P

LAYERS = 2
MESH = pl.DeviceIdType.MESH
F32 = jnp.float32
BF16 = jnp.bfloat16
NT = (((1,), (1,)), ((), ()))


def layer_norm(values, gain_vec, bias_vec):
    average = jnp.mean(values, axis=-1, keepdims=True)
    centred = values - average
    variance = jnp.mean(centred * centred, axis=-1, keepdims=True)
    return centred * lax.rsqrt(variance + 1e-05) * gain_vec + bias_vec


def peer_offsets(n_req, n_head):
    every = [(a, b) for a in range(n_req) for b in range(n_head) if a or b]
    return sorted(every, key=lambda o: (-(o[0] + bin(o[1] >> 1).count("1")), -o[1]))


def flip(index, mask):
    bit = 1
    while bit <= mask:
        if mask & bit:
            index = index + bit - 2 * bit * lax.rem(index // bit, 2)
        bit *= 2
    return index


def kernel(
    n_req,
    n_head,
    hidden_ref,
    lengths_ref,
    order_ref,
    key_hbm,
    value_hbm,
    qkv_hbm,
    out_w_hbm,
    up_hbm,
    bias_up_ref,
    down_hbm,
    gain_ref,
    bias_ref,
    emb_hbm,
    logits_ref,
    key_v,
    value_v,
    qkv_v,
    out_w_v,
    up_v,
    down_v,
    emb_v,
    load_sem,
    emb_sem,
    state_v,
    normed_v,
    first,
    attn_out,
    attn_in,
    spread,
    mlp_out,
    mlp_in,
    near,
    send_sem,
    recv_sem,
):
    me_r = lax.axis_index("req")
    me_h = lax.axis_index("head")
    me = me_r * n_head + me_h
    rows, width = hidden_ref.shape
    group, heads, head_size, cached = key_v.shape[1:]
    slots = n_req * group
    devices = n_req * n_head
    part = width // n_head
    offsets = peer_offsets(n_req, n_head)
    everywhere = [(flip(me_r, a), flip(me_h, b)) for a, b in offsets]
    plane = [(me_r, flip(me_h, b)) for a, b in offsets if not a]

    barrier = pltpu.get_barrier_semaphore()
    for peer in everywhere:
        pl.semaphore_signal(barrier, inc=1, device_id=peer, device_id_type=MESH)

    pairs = (
        (qkv_hbm, qkv_v),
        (key_hbm, key_v),
        (value_hbm, value_v),
        (out_w_hbm, out_w_v),
        (up_hbm, up_v),
        (down_hbm, down_v),
    )

    def load(layer, which):
        source, target = pairs[which]
        return pltpu.make_async_copy(source.at[layer], target.at[layer], load_sem.at[layer, which])

    for layer in range(LAYERS):
        for which in range(len(pairs)):
            load(layer, which).start()
    emb_load = pltpu.make_async_copy(emb_hbm, emb_v, emb_sem)
    emb_load.start()

    def send(turn, source, target, peers):
        for peer in peers:
            pltpu.make_async_remote_copy(
                src_ref=source(peer),
                dst_ref=target,
                send_sem=send_sem.at[turn],
                recv_sem=recv_sem.at[turn],
                device_id=peer,
                device_id_type=MESH,
            ).start()

    def wait(sem, turn, ref, count):
        block = ref.at[pl.ds(0, count)]
        pltpu.make_async_copy(block, block, sem.at[turn]).wait()

    chunks = width // 128
    tile = first.shape[1]
    hidden = hidden_ref[...].astype(F32)
    pieces = [hidden[:, c * 128 : (c + 1) * 128] for c in range(chunks)]
    if tile > chunks * rows:
        pieces.append(jnp.zeros((tile - chunks * rows, 128), F32))
    first[me] = jnp.concatenate(pieces, axis=0).astype(BF16)

    order_row = order_ref[...]
    ids_row = lax.broadcasted_iota(jnp.int32, (group, slots), 0) + me_r * group
    ids_col = lax.broadcasted_iota(jnp.int32, (group, slots), 1)
    order_here = jnp.sum(
        jnp.where(ids_row == ids_col, jnp.broadcast_to(order_row, (group, slots)).astype(F32), 0.0),
        axis=1,
        keepdims=True,
    ).astype(jnp.int32)
    wanted = (order_here // rows) * tile + lax.rem(order_here, rows)
    wide = lax.broadcasted_iota(jnp.int32, (group, devices * tile), 1)
    wanted = jnp.broadcast_to(wanted, (group, devices * tile))
    choose = jnp.concatenate(
        [(wide == wanted + c * rows).astype(F32) for c in range(chunks)], axis=0
    ).astype(BF16)

    row_ids = lax.broadcasted_iota(jnp.int32, (group, cached), 0)
    limit = jnp.zeros((group, cached), jnp.int32)
    for row in range(group):
        limit = jnp.where(row_ids == row, lengths_ref[row], limit)
    valid = lax.broadcasted_iota(jnp.int32, (group, cached), 1) < limit
    flat = group * head_size
    diagonal = lax.broadcasted_iota(jnp.int32, (group, flat), 0) == (
        lax.broadcasted_iota(jnp.int32, (group, flat), 1) // head_size
    )
    score_scale = head_size ** (-0.5)

    pl.semaphore_wait(barrier, devices - 1)
    send(0, lambda peer: first.at[me], first.at[me], everywhere)
    wait(recv_sem, 0, first, devices - 1)
    chosen = jnp.dot(choose, first[...].reshape(devices * tile, 128), preferred_element_type=F32)
    state = jnp.concatenate([chosen[c * group : (c + 1) * group] for c in range(chunks)], axis=1)
    for head in range(n_head):
        state_v[head] = state[:, head * part : (head + 1) * part].astype(BF16)

    def joined(ref, lead):
        return jnp.concatenate([ref[lead + (head,)] for head in range(n_head)], axis=1)

    def layer_step(layer, carry):
        attn_turn, spread_turn, mlp_turn, near_turn = 1 + 4 * layer, 2 + 4 * layer, 3 + 4 * layer, 4 + 4 * layer
        state = joined(state_v, ())
        load(layer, 0).wait()
        attn = jnp.zeros((group, width), F32)
        parts = []
        for head in range(heads):
            projected = (
                lax.dot_general(state, qkv_v[layer, head], NT, preferred_element_type=F32).astype(BF16).astype(F32)
            )
            parts.append(
                (
                    projected[:, :head_size],
                    projected[:, head_size : 2 * head_size],
                    projected[:, 2 * head_size :],
                )
            )
        load(layer, 1).wait()
        expos = []
        for head in range(heads):
            query, own_key, own_value = parts[head]
            tiled = jnp.where(diagonal, jnp.concatenate([query] * group, axis=1), 0.0).astype(BF16)
            keys = key_v[layer, :, head].reshape(flat, cached)
            scores = jnp.dot(tiled, keys, preferred_element_type=F32) * score_scale
            scores = jnp.where(valid, scores, -jnp.inf)
            own = jnp.sum(query * own_key, axis=-1, keepdims=True) * score_scale
            row_max = jnp.maximum(jnp.max(scores, axis=-1, keepdims=True), own)
            expo = jnp.exp(scores - row_max)
            own_exp = jnp.exp(own - row_max)
            denom = jnp.sum(expo, axis=-1, keepdims=True) + own_exp
            expos.append((expo.astype(BF16), own_exp.astype(BF16).astype(F32), denom))
        load(layer, 2).wait()
        load(layer, 3).wait()
        for head in range(heads):
            expo, own_exp, denom = expos[head]
            values = value_v[layer, :, head].reshape(flat, cached)
            every = lax.dot_general(expo, values, NT, preferred_element_type=F32)
            every = jnp.where(diagonal, every, 0.0)
            mixed = every[:, :head_size]
            for block in range(1, group):
                mixed += every[:, block * head_size : (block + 1) * head_size]
            mixed += own_exp * parts[head][2]
            head_out = (mixed / denom).astype(BF16)
            attn += jnp.dot(head_out, out_w_v[layer, head], preferred_element_type=F32)
        for head in range(n_head):
            attn_out[layer, head] = attn[:, head * part : (head + 1) * part].astype(BF16)
        send(attn_turn, lambda peer: attn_out.at[layer, peer[1]], attn_in.at[layer, me_h], plane)
        attn_in[layer, me_h] = attn_out[layer, me_h]
        wait(recv_sem, attn_turn, attn_in.at[layer], n_head - 1)
        total = attn_in[layer, 0].astype(F32)
        for head in range(1, n_head):
            total += attn_in[layer, head].astype(F32)
        spread[layer, me] = (total + state_v[me_h].astype(F32)).astype(BF16)
        send(spread_turn, lambda peer: spread.at[layer, me], spread.at[layer, me], everywhere)
        gains, biases = gain_ref[layer], bias_ref[layer]
        bias_up = bias_up_ref[...].astype(F32)
        bias_row = bias_up[0:1]
        for other in range(1, LAYERS):
            bias_row = jnp.where(layer == other, bias_up[other : other + 1], bias_row)
        load(layer, 4).wait()
        load(layer, 5).wait()
        wait(recv_sem, spread_turn, spread.at[layer], devices - 1)
        before = jnp.concatenate(
            [
                jnp.concatenate([spread[layer, req * n_head + head] for head in range(n_head)], axis=1)
                for req in range(n_req)
            ],
            axis=0,
        ).astype(F32)
        normed = layer_norm(before, gains[0:1], biases[0:1]).astype(BF16)
        for req in range(n_req):
            for head in range(n_head):
                normed_v[req * n_head + head] = normed[
                    req * group : (req + 1) * group, head * part : (head + 1) * part
                ]
        pre_act = jnp.dot(normed, up_v[layer], preferred_element_type=F32) + bias_row
        hidden = (0.5 * pre_act * (1.0 + lax.erf(pre_act * 0.7071067811865476))).astype(BF16)
        mlp = lax.dot_general(hidden, down_v[layer], NT, preferred_element_type=F32).astype(BF16)
        for req in range(n_req):
            for head in range(n_head):
                mlp_out[layer, req * n_head + head] = mlp[
                    req * group : (req + 1) * group, head * part : (head + 1) * part
                ]
        send(mlp_turn, lambda peer: mlp_out.at[layer, peer[0] * n_head + peer[1]], mlp_in.at[layer, me], everywhere)
        mlp_in[layer, me] = mlp_out[layer, me]
        wait(recv_sem, mlp_turn, mlp_in.at[layer], devices - 1)
        total = mlp_in[layer, 0].astype(F32)
        for device in range(1, devices):
            total += mlp_in[layer, device].astype(F32)
        after = (total + normed_v[me].astype(F32)).astype(BF16)

        @pl.when(layer < LAYERS - 1)
        def _():
            near[layer, me_h] = after
            send(near_turn, lambda peer: near.at[layer, me_h], near.at[layer, me_h], plane)
            wait(recv_sem, near_turn, near.at[layer], n_head - 1)
            fresh = joined(near, (layer,)).astype(F32)
            fresh = layer_norm(fresh, gains[1:2], biases[1:2]).astype(BF16)
            for head in range(n_head):
                state_v[head] = fresh[:, head * part : (head + 1) * part]

        @pl.when(layer == LAYERS - 1)
        def _():
            spread[LAYERS, me] = after

        return carry

    lax.fori_loop(0, LAYERS, layer_step, 0)
    last = 4 * LAYERS
    send(last, lambda peer: spread.at[LAYERS, me], spread.at[LAYERS, me], everywhere)
    pick = (
        (
            lax.broadcasted_iota(jnp.int32, (slots, slots), 0)
            == jnp.broadcast_to(order_row, (slots, slots))
        )
        .astype(F32)
        .astype(BF16)
    )
    emb_load.wait()
    wait(send_sem, 0, first, devices - 1)
    for layer in range(LAYERS):
        wait(send_sem, 1 + 4 * layer, attn_in.at[layer], n_head - 1)
        wait(send_sem, 2 + 4 * layer, spread.at[layer], devices - 1)
        wait(send_sem, 3 + 4 * layer, mlp_in.at[layer], devices - 1)
        if layer < LAYERS - 1:
            wait(send_sem, 4 + 4 * layer, near.at[layer], n_head - 1)
    wait(recv_sem, last, spread.at[LAYERS], devices - 1)
    before = jnp.concatenate(
        [
            jnp.concatenate([spread[LAYERS, req * n_head + head] for head in range(n_head)], axis=1)
            for req in range(n_req)
        ],
        axis=0,
    ).astype(F32)
    gains, biases = gain_ref[LAYERS - 1], bias_ref[LAYERS - 1]
    final = layer_norm(before, gains[1:2], biases[1:2]).astype(BF16)
    ordered = jnp.dot(pick, final, preferred_element_type=F32).astype(BF16)
    logits_ref[...] = lax.dot_general(ordered, emb_v[...], NT, preferred_element_type=F32)
    wait(send_sem, last, spread.at[LAYERS], devices - 1)


def body(n_req, n_head, *args):
    (hidden_in, lengths, request_order, key_cache, value_cache, w_qkv, w_out, w_up, bias_up, w_down) = args[:10]
    norm_gain, norm_bias, embedding = args[10:]
    group = lengths.shape[0]
    width = hidden_in.shape[1]
    w_qkv = jnp.swapaxes(w_qkv, 2, 3)
    slots = request_order.shape[0]
    devices = n_req * n_head
    part = width // n_head
    tile = max(16, hidden_in.shape[0] * width // 128)
    vmem = pl.BlockSpec(memory_space=pltpu.VMEM)
    smem = pl.BlockSpec(memory_space=pltpu.SMEM)
    hbm = pl.BlockSpec(memory_space=pl.ANY)
    dma = pltpu.SemaphoreType.DMA
    held = [key_cache, value_cache, w_qkv, w_out, w_up, w_down, embedding]
    return pl.pallas_call(
        functools.partial(kernel, n_req, n_head),
        out_shape=jax.ShapeDtypeStruct((slots, embedding.shape[0]), F32),
        in_specs=[vmem, smem, vmem, hbm, hbm, hbm, hbm, hbm, vmem, hbm, vmem, vmem, hbm],
        out_specs=vmem,
        scratch_shapes=[pltpu.VMEM(array.shape, array.dtype) for array in held]
        + [
            dma((LAYERS, 6)),
            dma,
            pltpu.VMEM((n_head, group, part), BF16),
            pltpu.VMEM((devices, group, part), BF16),
            pltpu.VMEM((devices, tile, 128), BF16),
            pltpu.VMEM((LAYERS, n_head, group, part), BF16),
            pltpu.VMEM((LAYERS, n_head, group, part), BF16),
            pltpu.VMEM((1 + LAYERS, devices, group, part), BF16),
            pltpu.VMEM((LAYERS, devices, group, part), BF16),
            pltpu.VMEM((LAYERS, devices, group, part), BF16),
            pltpu.VMEM((LAYERS, n_head, group, part), BF16),
            dma((1 + 4 * LAYERS,)),
            dma((1 + 4 * LAYERS,)),
        ],
        compiler_params=pltpu.CompilerParams(
            collective_id=0, has_side_effects=True, vmem_limit_bytes=56 * 1024 * 1024
        ),
    )(
        hidden_in,
        lengths,
        request_order.reshape(1, slots),
        key_cache,
        value_cache,
        w_qkv,
        w_out,
        w_up,
        bias_up,
        w_down,
        norm_gain,
        norm_bias,
        embedding,
    )


def solution(mesh):
    placed = (
        P(("req", "head"), None),
        P("req"),
        P(),
        P(None, "req", "head", None, None),
        P(None, "req", "head", None, None),
        P(None, "head", None, None),
        P(None, "head", None, None),
        P(None, None, ("req", "head")),
        P(None, ("req", "head")),
        P(None, None, ("req", "head")),
        P(),
        P(),
        P(("req", "head"), None),
    )
    return jax.shard_map(
        functools.partial(body, mesh.shape["req"], mesh.shape["head"]),
        mesh=mesh,
        in_specs=placed,
        out_specs=P(None, ("req", "head")),
        check_vma=False,
    )
```

time: 69.6 us -> 57 us (0.82)
  Pallas kernels: 63.8 us -> 55 us
  local copies, waits for them, and re-layouts: 5.52 us -> 1.77 us
    pallas_call x1, Pallas kernels: 63.8 us -> 55 us  [body(): pl.pallas_call(functools.partial(kernel, n_req, n_head), out_shape=jax.Sh...]
    unnamed x2 -> x1, local copies, waits for them, and re-layouts: 5.52 us -> 1.77 us
where the time goes in v2:
time: 57 us; the launch traced here: 56.8 us
  Pallas kernels  55 us (96%)
  local copies, waits for them, and re-layouts  1.77 us (3%)
    pallas_call x1, Pallas kernels, body(): pl.pallas_call(functools.partial(kernel, n_req, n_head), out_shape=jax.Sh...  55 us
    unnamed x1, local copies, waits for them, and re-layouts  1.77 us

profile of v2, /device:TPU:0, one launch (start us, length us, event | category | flops | bytes accessed | tf_op | source)
XLA Modules:
  0.0 56.8 jit_solution(11033106589618714869)
XLA Ops:
  0.0 55.0 %shard_map.127 = f32[64,1536]{1,0:T(8,128)} custom-call(bf16[2,1024]{1,0:T(2,128)(2,1)} %hidden_ref.1, s32[16]{0:T(128)} %lengths_ref.1, s32[1,64]{1,0:T(1,128)} %bitcast.3, bf16[2,16,2,64,1024]{4,3,2,1,0:T(8,128)(2,1)} %key_hbm.1, bf16[2,16,2,64,1024]{4,3,2,1,0:T(8,128)(2,1)} %value_hbm.1, bf16[2,2,192,1024]{3,2,1,0:T(8,128)(2,1)} %bitcast.2, ...), custom_call_target="tpu_custom_call" | custom-call | tf_op jit(solution)/shard_map/pallas_call | solution.py:327
  55.0 1.8 %copy.15 = f32[64,1536]{1,0:T(8,128)} copy(f32[64,1536]{1,0:T(8,128)} %shard_map.127) | data formatting | bytes 786432

commit v3 on v2

--- a/solution.py
+++ b/solution.py
@@ -146,10 +146,13 @@
         [(wide == wanted + c * rows).astype(F32) for c in range(chunks)], axis=0
     ).astype(BF16)
 
-    row_ids = lax.broadcasted_iota(jnp.int32, (group, cached), 0)
-    limit = jnp.zeros((group, cached), jnp.int32)
-    for row in range(group):
-        limit = jnp.where(row_ids == row, lengths_ref[row], limit)
+    square = lax.broadcasted_iota(jnp.int32, (group, group), 0) == lax.broadcasted_iota(
+        jnp.int32, (group, group), 1
+    )
+    limit = jnp.sum(
+        jnp.where(square, jnp.broadcast_to(lengths_ref[...], (group, group)).astype(F32), 0.0), axis=1, keepdims=True
+    ).astype(jnp.int32)
+    limit = jnp.broadcast_to(limit, (group, cached))
     valid = lax.broadcasted_iota(jnp.int32, (group, cached), 1) < limit
     flat = group * head_size
     diagonal = lax.broadcasted_iota(jnp.int32, (group, flat), 0) == (
@@ -320,14 +323,14 @@
     part = width // n_head
     tile = max(16, hidden_in.shape[0] * width // 128)
     vmem = pl.BlockSpec(memory_space=pltpu.VMEM)
-    smem = pl.BlockSpec(memory_space=pltpu.SMEM)
-    hbm = pl.BlockSpec(memory_space=pl.ANY)
+    hbm = pl.BlockSpec(memory_space=pltpu.HBM)
     dma = pltpu.SemaphoreType.DMA
+    pin = lambda array: pltpu.with_memory_space_constraint(array, pltpu.HBM)
     held = [key_cache, value_cache, w_qkv, w_out, w_up, w_down, embedding]
     return pl.pallas_call(
         functools.partial(kernel, n_req, n_head),
         out_shape=jax.ShapeDtypeStruct((slots, embedding.shape[0]), F32),
-        in_specs=[vmem, smem, vmem, hbm, hbm, hbm, hbm, hbm, vmem, hbm, vmem, vmem, hbm],
+        in_specs=[vmem] * 3 + [hbm] * 5 + [vmem, hbm, vmem, vmem, hbm],
         out_specs=vmem,
         scratch_shapes=[pltpu.VMEM(array.shape, array.dtype) for array in held]
         + [
@@ -346,22 +349,22 @@
             dma((1 + 4 * LAYERS,)),
         ],
         compiler_params=pltpu.CompilerParams(
-            collective_id=0, has_side_effects=True, vmem_limit_bytes=56 * 1024 * 1024
+            collective_id=0, has_side_effects=True, vmem_limit_bytes=40 * 1024 * 1024
         ),
     )(
-        hidden_in,
-        lengths,
-        request_order.reshape(1, slots),
-        key_cache,
-        value_cache,
-        w_qkv,
-        w_out,
-        w_up,
-        bias_up,
-        w_down,
-        norm_gain,
-        norm_bias,
-        embedding,
+        pin(hidden_in),
+        pin(lengths.reshape(1, group)),
+        pin(request_order.reshape(1, slots)),
+        pin(key_cache),
+        pin(value_cache),
+        pin(w_qkv),
+        pin(w_out),
+        pin(w_up),
+        pin(bias_up),
+        pin(w_down),
+        pin(norm_gain),
+        pin(norm_bias),
+        pin(embedding),
     )
 
 

time: 57 us -> 55.2 us (0.968)
  local copies, waits for them, and re-layouts: 1.77 us -> 0.75 us
  Pallas kernels: 55 us -> 54.2 us
    unnamed x1, local copies, waits for them, and re-layouts: 1.77 us -> 0.75 us
    pallas_call x1, Pallas kernels: 55 us -> 54.2 us  [body(): pl.pallas_call(functools.partial(kernel, n_req, n_head), out_shape=jax.Sh...]
where the time goes in v3:
time: 55.2 us; the launch traced here: 55 us
  Pallas kernels  54.2 us (98%)
  local copies, waits for them, and re-layouts  0.75 us (1%)
    pallas_call x1, Pallas kernels, body(): pl.pallas_call(functools.partial(kernel, n_req, n_head), out_shape=jax.Sh...  54.2 us

profile of v3, /device:TPU:0, one launch (start us, length us, event | category | flops | bytes accessed | tf_op | source)
XLA Modules:
  0.0 55.0 jit_solution(10424908128012740491)
XLA Ops:
  0.0 54.2 %shard_map.127 = f32[64,1536]{1,0:T(8,128)S(1)} custom-call(bf16[2,1024]{1,0:T(2,128)(2,1)} %hidden_ref.1, s32[1,16]{1,0:T(1,128)} %bitcast.4, s32[1,64]{1,0:T(1,128)} %bitcast.5, bf16[2,16,2,64,1024]{4,3,2,1,0:T(8,128)(2,1)} %key_hbm.1, bf16[2,16,2,64,1024]{4,3,2,1,0:T(8,128)(2,1)} %value_hbm.1, bf16[2,2,192,1024]{3,2,1,0:T(8,128)(2,1)} %bitcast.3, ...), custom_call_target="tpu_custom_call" | custom-call | tf_op jit(solution)/shard_map/pallas_call | solution.py:330
  54.2 0.7 %copy.15 = f32[64,1536]{1,0:T(8,128)} copy(f32[64,1536]{1,0:T(8,128)S(1)} %shard_map.127) | data formatting | bytes 786432
